TPU v7x, 128 devices: a whole 4x4x4 slice. The times are simulated.
128 devices in a mesh: tok: 8 (over z, core), head: 16 (over y, x).
Axes of the slice: x: 4, y: 4, z: 4, core: 2. Of those that a mesh axis runs over, the one named last changes fastest.
Arguments:
- stream: bfloat16 [2048, 7168], P('tok'), may hold values from -400 to 400
- row_tree_nodes: int32 [2048], replicated, may hold values from 0 to 2047, as said below
- input_norm_gain: bfloat16 [7168], replicated, may hold values from 0.099609375 to 1.8984375
- query_key_value_weight: bfloat16 [7168, 3, 7168], P('head', None, 'tok'), may hold values from -0.141736677 to 0.141736677
- adapter_down_weight: bfloat16 [7168, 128], replicated, may hold values from -0.0625 to 0.0625
- adapter_up_weight: bfloat16 [128, 3, 7168], P('head', None, 'tok'), may hold values from -0.23925781 to 0.23925781
- key_value_cache: bfloat16 [2, 32, 2048, 7168], P(None, 'head', None, 'tok'), may hold values from -104 to 104
- cache_length: int32 [32], P('head'), may hold values from 256 to 2048, as said below
- parents: int32 [32, 64], P('head'), may hold values from 0 to 62, as said below
- accepted: int32 [32, 8], P('head'), may hold values from 0 to 63, as said below
- output_weight: bfloat16 [7168, 3584], P('tok', 'head'), may hold values from -0.375 to 0.375
Outputs:
- attended: bfloat16 [2048, 3584], P('tok', 'head')
- accepted_kv: bfloat16 [2, 32, 8, 7168], P(None, 'head', None, 'tok')
Inputs may be any that keep to these rules, and one draw needn't show every extreme that they name: row_tree_nodes is a permutation of the 2048 node numbers; every aligned block of 128 rows holds exactly 4 nodes of every request. `cache_length`: at least one request's cache holds exactly 2048 positions. parents[r, 0] = 0 marks the root; parents[r, n] < n for n > 0. `accepted`: each row lists 8 nodes of its request's tree, each the parent of the next.
All inputs are finite; a program needn't handle non-finite values.
Results may differ from a plain program's by a relative error of at most 0.014.
Values may be sent and summed in bfloat16 or wider, within the bound.
A program may use at most 192 MiB of HBM per device.

v0:
```python
import jax
import jax.numpy as jnp
from jax import lax
from jax.sharding import PartitionSpec as P

HEAD_SIZE = 224
NODES = 64


def ancestors_of(parents):
    parent_links = jax.nn.one_hot(parents, NODES, dtype=jnp.float32)
    identity_matrix = jnp.eye(NODES, dtype=jnp.float32)
    ancestry = jnp.minimum(identity_matrix[None] + parent_links, 1.0)
    for squaring in range(NODES.bit_length()):
        ancestry = jnp.minimum(
            jnp.einsum("rnm,rmk->rnk", ancestry, ancestry, precision=lax.Precision.HIGHEST), 1.0
        )
    return ancestry


def on_device(
    stream,
    row_tree_nodes,
    input_norm_gain,
    query_key_value_weight,
    adapter_down_weight,
    adapter_up_weight,
    key_value_cache,
    cache_length,
    parents,
    accepted,
    output_weight,
):
    owner_index = lax.axis_index("head")
    feature_rows = query_key_value_weight.shape[0]
    device_width = query_key_value_weight.shape[2]
    adapter_rank_rows = adapter_up_weight.shape[0]
    local_heads = device_width // HEAD_SIZE
    request_count = key_value_cache.shape[1]
    cache_span = key_value_cache.shape[2]
    wide_rows = stream.astype(jnp.float32)
    inverse_rms = lax.rsqrt(jnp.mean(wide_rows * wide_rows, axis=1, keepdims=True) + 1e-05)
    normalized_input = (wide_rows * inverse_rms * input_norm_gain.astype(jnp.float32)).astype(
        jnp.bfloat16
    )
    reduced_rank_rows = jnp.dot(
        normalized_input, adapter_down_weight, preferred_element_type=jnp.float32
    ).astype(jnp.bfloat16)
    feature_block = lax.dynamic_slice_in_dim(
        normalized_input, owner_index * feature_rows, feature_rows, 1
    )
    rank_block = lax.dynamic_slice_in_dim(
        reduced_rank_rows, owner_index * adapter_rank_rows, adapter_rank_rows, 1
    )
    gathered_features, gathered_ranks = (
        lax.all_gather(feature_block, "tok", axis=0, tiled=True),
        lax.all_gather(rank_block, "tok", axis=0, tiled=True),
    )
    projection = query_key_value_weight.reshape(feature_rows, 3 * device_width)
    lifting_matrix = adapter_up_weight.reshape(adapter_rank_rows, 3 * device_width)
    node_to_row = jnp.argsort(row_tree_nodes)
    part_sum = jnp.dot(
        gathered_features[node_to_row], projection, preferred_element_type=jnp.float32
    )
    node_rows = lax.psum_scatter(
        part_sum
        + jnp.dot(gathered_ranks[node_to_row], lifting_matrix, preferred_element_type=jnp.float32),
        "head",
        scatter_dimension=0,
        tiled=True,
    ).astype(jnp.bfloat16)
    triple = node_rows.reshape(request_count, NODES, 3, local_heads, HEAD_SIZE)
    queries = triple[:, :, 0]
    tree_key_rows = triple[:, :, 1]
    tree_value_rows = triple[:, :, 2]
    ancestry = ancestors_of(parents)
    attention_score_scale = HEAD_SIZE ** (-0.5)
    tree_score_matrix = (
        jnp.einsum("rnhd,rmhd->rhnm", queries, tree_key_rows, preferred_element_type=jnp.float32)
        * attention_score_scale
    )
    tree_score_matrix = jnp.where(ancestry[:, None] > 0.5, tree_score_matrix, -jnp.inf)
    keys_cache = key_value_cache[0].reshape(request_count, cache_span, local_heads, HEAD_SIZE)
    values_cache = key_value_cache[1].reshape(request_count, cache_span, local_heads, HEAD_SIZE)
    scores = (
        jnp.einsum("rnhd,rchd->rhnc", queries, keys_cache, preferred_element_type=jnp.float32)
        * attention_score_scale
    )
    positions = lax.broadcasted_iota(jnp.int32, (1, 1, 1, cache_span), 3)
    scores = jnp.where(positions < cache_length[:, None, None, None], scores, -jnp.inf)
    tree_top = jnp.max(tree_score_matrix, axis=-1, keepdims=True)
    largest = jnp.maximum(tree_top, jnp.max(scores, axis=-1, keepdims=True))
    cache_exp = jnp.exp(scores - largest)
    tree_exp = jnp.exp(tree_score_matrix - largest)
    totals = jnp.sum(cache_exp, axis=-1, keepdims=True) + jnp.sum(tree_exp, axis=-1, keepdims=True)
    cache_weights = (cache_exp / totals).astype(jnp.bfloat16)
    tree_weight_matrix = (tree_exp / totals).astype(jnp.bfloat16)
    attention = jnp.einsum(
        "rhnc,rchd->rnhd", cache_weights, values_cache, preferred_element_type=jnp.float32
    )
    attention = attention + jnp.einsum(
        "rhnm,rmhd->rnhd", tree_weight_matrix, tree_value_rows, preferred_element_type=jnp.float32
    )
    head_rows = attention.astype(jnp.bfloat16).reshape(request_count * NODES, device_width)
    node_table = node_rows.reshape(request_count, NODES, 3, device_width)
    chosen = jnp.take_along_axis(node_table, accepted[:, :, None, None], axis=1)
    accepted_kv = jnp.stack([chosen[:, :, 1], chosen[:, :, 2]])
    everything = lax.all_gather(head_rows, "head", axis=0, tiled=True)
    attended = lax.psum_scatter(
        jnp.dot(
            everything[row_tree_nodes], output_weight, preferred_element_type=jnp.float32
        ).astype(jnp.bfloat16),
        "tok",
        scatter_dimension=0,
        tiled=True,
    )
    return (attended, accepted_kv)


def solution(mesh):
    placed = (
        P("tok", None),
        P(),
        P(),
        P("head", None, "tok"),
        P(),
        P("head", None, "tok"),
        P(None, "head", None, "tok"),
        P("head"),
        P("head", None),
        P("head", None),
        P("tok", "head"),
    )
    return jax.shard_map(
        on_device,
        mesh=mesh,
        in_specs=placed,
        out_specs=(P("tok", "head"), P(None, "head", None, "tok")),
        check_vma=False,
    )
```

profile of v0, /device:TPU:0, one launch (start us, length us, event | category | flops | bytes accessed | tf_op | source)
XLA Modules:
  0.0 344.5 jit_solution(10668677327071454545)
XLA Ops:
  7.2 0.8 convert_element_type.39
  8.1 2.8 fusion
  10.9 3.1 fusion.2
  14.0 1.8 copy-done.2
  15.8 0.9 constant_dynamic-slice_fusion
  16.7 4.5 %copy.21 = bf16[448,3,896]{0,2,1:T(8,128)(2,1)} copy(bf16[448,3,896]{2,0,1:T(8,128)(2,1)} %param.14) | data formatting | bytes 4816896 | tf_op args[3]
  21.2 5.0 %sort.17 = (s32[2048]{0:T(1024)}, s32[2048]{0:T(1024)S(1)}) sort(s32[2048]{0:T(1024)S(1)} %copy-done.4, s32[2048]{0:T(1024)S(1)} %iota.34), dimensions={0}, to_apply=%region_1.0 | sort | flops 22528 | bytes 32768 | tf_op jit(solution)/shard_map/jit(argsort)/sort | solution.py:61
  26.3 3.2 fusion.32
  29.6 15.4 %all_gather.10 = bf16[2048,8]{1,0:T(8,128)(2,1)S(1)} all-gather(bf16[256,8]{1,0:T(8,128)(2,1)S(1)} %dynamic-slice_convert_fusion), channel_id=1, replica_groups=mesh['tok'=8,'head'=16] {'tok'}, dimensions={0}, use_global_device_ids=true | all-gather | bytes 36864 | tf_op jit(solution)/shard_map/all_gather | solution.py:57
  45.0 6.2 %gather_fusion.1 = bf16[2048,8]{1,0:T(8,128)(2,1)S(1)} fusion(bf16[2048,8]{1,0:T(8,128)(2,1)S(1)} %all_gather.10, s32[2048]{0:T(1024)S(1)} %fusion.23), kind=kCustom, calls=%fused_computation.1 | custom fusion | bytes 73728 | tf_op jit(solution)/shard_map/gather | solution.py:67
  51.2 11.1 %gather_fusion = bf16[2048,448]{1,0:T(8,128)(2,1)} fusion(bf16[2048,448]{1,0:T(8,128)(2,1)} %all-gather.3.cloned.1.call-done, s32[2048]{0:T(1024)S(1)} %fusion.23), kind=kCustom, calls=%fused_computation | custom fusion | bytes 3678208 | tf_op jit(solution)/shard_map/gather | solution.py:63
  62.3 12.6 %fusion.31 = f32[2048,2688]{1,0:T(8,128)} fusion(bf16[2048,448]{1,0:T(8,128)(2,1)} %gather_fusion, bf16[448,2688]{0,1:T(8,128)(2,1)} %bitcast.63), kind=kOutput, calls=%fused_computation.71 | convolution fusion | flops 4932501504 | bytes 26263552 | tf_op jit(solution)/shard_map/dot_general | solution.py:62
  74.9 14.2 %convolution_add_fusion = f32[2048,2688]{1,0:T(8,128)} fusion(f32[2048,2688]{1,0:T(8,128)} %fusion.31, bf16[2048,8]{1,0:T(8,128)(2,1)S(1)} %gather_fusion.1, bf16[8,2688]{1,0:T(8,128)(2,1)S(1)} %bitcast.65), kind=kOutput, calls=%fused_computation.4 | convolution fusion | flops 93585408 | bytes 44115968 | tf_op jit(solution)/shard_map/dot_general | solution.py:67
  89.4 0.4 copy-done.5
  89.8 0.3 convolution_minimum_fusion.6
  91.4 10.6 %fusion.28 = (bf16[1,2,2048,896]{3,2,1,0:T(8,128)(2,1)}, bf16[1,2,2048,896]{3,2,1,0:T(8,128)(2,1)}) fusion(bf16[2,2,2048,896]{3,2,1,0:T(8,128)(2,1)} %param.17), kind=kLoop, calls=%fused_computation.68 | loop fusion | bytes 29360128 | tf_op jit(solution)/shard_map/slice | solution.py:83
  102.0 11.3 %copy.23 = bf16[1,2,2048,896]{2,3,1,0:T(8,128)(2,1)} copy(bf16[1,2,2048,896]{3,2,1,0:T(8,128)(2,1)} %get-tuple-element.4) | data formatting | bytes 14680064 | tf_op jit(solution)/shard_map/slice | solution.py:83
  113.3 11.6 %copy.26 = bf16[1,2,2048,896]{2,3,1,0:T(8,128)(2,1)} copy(bf16[1,2,2048,896]{3,2,1,0:T(8,128)(2,1)} %get-tuple-element.5) | data formatting | bytes 14680064 | tf_op jit(solution)/shard_map/slice | solution.py:84
  124.9 102.2 %reduce-scatter.3.cloned.1.call-done = f32[128,2688]{1,0:T(8,128)} async-done(((f32[2048,2688]{1,0:T(8,128)}), f32[128,2688]{1,0:T(8,128)}) %reduce-scatter.3.cloned.1.call-update) | async-done | bytes 1376272 | tf_op jit(solution)/shard_map/reduce_scatter | solution.py:65
  227.2 1.4 convert_element_type.42
  228.6 0.9 reshape.94
  230.0 4.8 %fusion.3 = (f32[2,4,64]{2,1,0:T(4,128)S(1)}, f32[2,4,64,2048]{3,2,1,0:T(8,128)S(1)}) fusion(pred[2,2048]{1,0:T(4,128)(4,1)S(1)} %iota_compare_fusion.3, bf16[2,2048,4,224]{1,3,2,0:T(8,128)(2,1)} %bitcast.59, bf16[2,64,1,4,224]{4,3,2,1,0:T(4,128)(2,1)S(1)} %get-tuple-element.8), kind=kOutput, calls=%fused_computation.13 | convolution fusion | flops 472907264 | bytes 11769856 | tf_op jit(solution)/shard_map/rnhd,rchd->rhnc/dot_general | solution.py:86
  234.9 1.0 fusion.4
  236.0 2.5 fusion.8
  238.4 0.3 fusion.9
  238.9 0.9 reshape.95
  239.9 49.4 %all-gather.5.cloned.1.call-done = bf16[2048,896]{1,0:T(8,128)(2,1)} async-done(((bf16[128,896]{1,0:T(8,128)(2,1)}), bf16[2048,896]{1,0:T(8,128)(2,1)}) %all-gather.5.cloned.1.call-update) | async-done | bytes 3670032 | tf_op jit(solution)/shard_map/all_gather | solution.py:108
  289.3 13.1 %gather_fusion.2 = bf16[2048,896]{1,0:T(8,128)(2,1)} fusion(bf16[2048,896]{1,0:T(8,128)(2,1)} %all-gather.5.cloned.1.call-done, s32[2048]{0:T(1024)S(1)} %fusion.24), kind=kCustom, calls=%fused_computation.2 | custom fusion | bytes 7348224 | tf_op jit(solution)/shard_map/gather | solution.py:111
  302.4 4.3 %convolution_convert_fusion = bf16[2048,224]{0,1:T(8,128)(2,1)} fusion(bf16[2048,896]{1,0:T(8,128)(2,1)} %gather_fusion.2, bf16[896,224]{0,1:T(8,128)(2,1)S(1)} %copy-done.8), kind=kOutput, calls=%fused_computation.15 | convolution fusion | flops 822542336 | bytes 4988928 | tf_op jit(solution)/shard_map/dot_general | solution.py:110
  307.1 0.7 gather_fusion.3
  307.9 0.6 pad_maximum_fusion
  308.5 29.4 %reduce-scatter.5.cloned.1.call-done = bf16[256,224]{0,1:T(8,128)(2,1)} async-done(((bf16[2048,224]{0,1:T(8,128)(2,1)}), bf16[256,224]{0,1:T(8,128)(2,1)}) %reduce-scatter.5.cloned.1.call-update) | async-done | bytes 114704 | tf_op jit(solution)/shard_map/reduce_scatter | solution.py:109
  (56 shorter events, 3.1 us)
Async XLA Ops:
  7.2 19.1 %copy-start = (bf16[7168,128]{1,0:T(8,128)(2,1)S(1)}, bf16[7168,128]{1,0:T(8,128)(2,1)}, u32[]{:S(2)}) copy-start(bf16[7168,128]{1,0:T(8,128)(2,1)} %param.15) | copy-start | bytes 5505028
  7.2 44.0 %all-gather.3.cloned.1.call-start = ((), (), s32[]{:S(2)}) async-start(), calls=%async_computation.2 | async-start | bytes 2359296 | tf_op jit(solution)/shard_map/all_gather | solution.py:56
  14.0 1.8 copy-start.2
  15.8 5.4 %copy-start.4 = (s32[2048]{0:T(1024)S(1)}, s32[2048]{0:T(1024)}, u32[]{:S(2)}) copy-start(s32[2048]{0:T(1024)} %param.12) | copy-start | bytes 24580
  16.7 210.5 %reduce-scatter.3.cloned.1.call-start = ((), (), s32[]{:S(2)}) async-start(), calls=%async_computation.3 | async-start | bytes 23396352 | tf_op jit(solution)/shard_map/reduce_scatter | solution.py:65
  62.3 12.6 %copy-start.3 = (bf16[8,3,896]{2,0,1:T(8,128)(2,1)S(1)}, bf16[8,3,896]{2,0,1:T(8,128)(2,1)}, u32[]{:S(2)}) copy-start(bf16[8,3,896]{2,0,1:T(8,128)(2,1)} %param.16) | copy-start | bytes 129028
  89.1 0.7 copy-start.5
  89.1 200.2 %all-gather.5.cloned.1.call-start = ((), (), s32[]{:S(2)}) async-start(), calls=%async_computation.4 | async-start | bytes 3899392 | tf_op jit(solution)/shard_map/all_gather | solution.py:108
  113.3 11.6 %copy-start.7 = (s32[2]{0:T(128)S(1)}, s32[2]{0:T(128)}, u32[]{:S(2)}) copy-start(s32[2]{0:T(128)} %param.18) | copy-start | bytes 28
  230.0 6.0 %slice-start = ((s8[7340032]{0:T(1024)(128)(4,1)}), s8[4194304]{0:T(1024)(128)(4,1)S(1)}, s32[]{:S(2)}) async-start(s8[7340032]{0:T(1024)(128)(4,1)} %bitcast.60), calls=%async_computation.6 | async-start | bytes 8388608
  230.0 5.9 %slice-start.1 = ((s8[7340032]{0:T(1024)(128)(4,1)}), s8[3145728]{0:T(1024)(128)(4,1)S(1)}, s32[]{:S(2)}) async-start(s8[7340032]{0:T(1024)(128)(4,1)} %bitcast.60), calls=%async_computation.7 | async-start | bytes 6291456
  239.8 98.1 %reduce-scatter.5.cloned.1.call-start = ((), (), s32[]{:S(2)}) async-start(), calls=%async_computation.5 | async-start | bytes 1032192 | tf_op jit(solution)/shard_map/reduce_scatter | solution.py:109
  239.9 62.5 %copy-start.8 = (bf16[896,224]{0,1:T(8,128)(2,1)S(1)}, bf16[896,224]{0,1:T(8,128)(2,1)}, u32[]{:S(2)}) copy-start(bf16[896,224]{0,1:T(8,128)(2,1)} %param.21) | copy-start | bytes 1204228
  289.3 48.7 %copy-start.1 = (bf16[7168,128]{1,0:T(8,128)(2,1)S(1)}, bf16[7168,128]{1,0:T(8,128)(2,1)}, u32[]{:S(2)}) copy-start(bf16[7168,128]{1,0:T(8,128)(2,1)} %param.15) | copy-start | bytes 5505028
  302.4 4.4 %copy-start.6 = (s32[2,8]{1,0:T(2,128)S(1)}, s32[2,8]{1,0:T(2,128)}, u32[]{:S(2)}) copy-start(s32[2,8]{1,0:T(2,128)} %param.20) | copy-start | bytes 196
Sparse Core Ops, SparseCore 0:
  16.8 28.7 all-gather.2
  89.3 137.8 reduce-scatter.2
  240.0 49.2 all-gather.4
  306.9 31.0 reduce-scatter.4
where the time goes:
time: 345 us; the launch traced here: 344 us
  waiting for transfers between devices  181 us (52%)
  local copies, waits for them, and re-layouts  74.8 us (22%)
  matrix products  43.6 us (13%)
  blocking collectives  15.4 us (4%)
  other arithmetic  15.2 us (4%)
  between operations  14 us (4%)
    reduce_scatter x1, waiting for transfers between devices, on_device(): lax.psum_scatter(part_sum + jnp.dot(gathered_ranks[node_to_row], lifting_...  102 us
    all_gather x1, waiting for transfers between devices, on_device(): everything = lax.all_gather(head_rows, 'head', axis=0, tiled=True)  49.4 us
    reduce_scatter x1, waiting for transfers between devices, on_device(): lax.psum_scatter(jnp.dot(everything[row_tree_nodes], output_weight, prefe...  29.4 us
    slice x2, local copies, waits for them, and re-layouts, on_device(): key_value_cache[0]  21.9 us
    all_gather x1, blocking collectives, on_device(): lax.all_gather(rank_block, 'tok', axis=0, tiled=True)  15.4 us
    dot_general x1, matrix products, on_device(): jnp.dot(gathered_ranks[node_to_row], lifting_matrix, preferred_element_ty...  14.2 us
    gather x1, local copies, waits for them, and re-layouts, on_device(): everything[row_tree_nodes]  13.1 us
    dot_general x1, matrix products, on_device(): jnp.dot(gathered_features[node_to_row], projection, preferred_element_typ...  12.6 us
  transfers between devices with their start and end apart: 4, of which 3 were waited for; matrix products, arithmetic and copies ran while one was open for 16% of the time, Pallas kernels for 0%

commit v1 on v0

--- a/solution.py
+++ b/solution.py
@@ -2,6 +2,7 @@
 import jax.numpy as jnp
 from jax import lax
 from jax.sharding import PartitionSpec as P
+from jax.lax import axis_index, axis_size, ppermute
 
 HEAD_SIZE = 224
 NODES = 64
@@ -31,6 +32,22 @@
     accepted,
     output_weight,
 ):
+
+    def _shape_teams(inner_x):
+        across = "tok"
+        count_all = axis_size(across)
+        nodes = [(rr, (rr + 1) % count_all) for rr in range(count_all)]
+        stack_in = [(rr, (rr - 1) % count_all) for rr in range(count_all)]
+        side_arr, newest = ([inner_x], [inner_x])
+        for _ in range(count_all // 2):
+            side_arr.append(ppermute(side_arr[-1], across, nodes))
+        for _ in [*range((count_all - 1) // 2)]:
+            newest.append(ppermute(newest[-1], across, stack_in))
+        view_out = jnp.concatenate([*side_arr[::-1], *newest[1:]], axis=0)
+        return jnp.roll(
+            view_out, shift=(axis_index(across) - count_all // 2) * inner_x.shape[0], axis=0
+        )
+
     owner_index = lax.axis_index("head")
     feature_rows = query_key_value_weight.shape[0]
     device_width = query_key_value_weight.shape[2]
@@ -54,7 +71,7 @@
     )
     gathered_features, gathered_ranks = (
         lax.all_gather(feature_block, "tok", axis=0, tiled=True),
-        lax.all_gather(rank_block, "tok", axis=0, tiled=True),
+        _shape_teams(rank_block),
     )
     projection = query_key_value_weight.reshape(feature_rows, 3 * device_width)
     lifting_matrix = adapter_up_weight.reshape(adapter_rank_rows, 3 * device_width)

time: 345 us -> 348 us (level)
  blocking collectives: 15.4 us -> 0 us
  starting transfers between devices: 0.34 us -> 9.17 us
  waiting for transfers between devices: 181 us -> 189 us
    all_gather x1 -> x0, blocking collectives: 15.4 us -> none  [on_device(): lax.all_gather(rank_block, 'tok', axis=0, tiled=True)]
    ppermute x0 -> x7, starting transfers between devices: none -> 8.83 us  [the longest x3 8.8 us: _shape_teams(): newest.append(ppermute(newest[-1], across, stack_in))]
    ppermute x0 -> x7, waiting for transfers between devices: none -> 7.4 us  [the longest x4 6.13 us: _shape_teams(): side_arr.append(ppermute(side_arr[-1], across, nodes))]
  transfers between devices with their start and end apart: 4 -> 11, of which waited for: 3 -> 6; matrix products, arithmetic and copies ran while one was open for 16% -> 16% of each run, Pallas kernels for 0% -> 0%
where the time goes in v1:
time: 348 us; the launch traced here: 347 us
  waiting for transfers between devices  189 us (54%)
  local copies, waits for them, and re-layouts  74.5 us (21%)
  matrix products  43.8 us (13%)
  other arithmetic  16.9 us (5%)
  between operations  14.1 us (4%)
  starting transfers between devices  9.17 us (3%)
    reduce_scatter x1, waiting for transfers between devices, on_device(): lax.psum_scatter(part_sum + jnp.dot(gathered_ranks[node_to_row], lifting_...  103 us
    all_gather x1, waiting for transfers between devices, on_device(): everything = lax.all_gather(head_rows, 'head', axis=0, tiled=True)  49.4 us
    reduce_scatter x1, waiting for transfers between devices, on_device(): lax.psum_scatter(jnp.dot(everything[row_tree_nodes], output_weight, prefe...  29.4 us
    slice x2, local copies, waits for them, and re-layouts, on_device(): key_value_cache[0]  22.1 us
    dot_general x1, matrix products, on_device(): jnp.dot(gathered_ranks[node_to_row], lifting_matrix, preferred_element_ty...  14.3 us
    gather x1, local copies, waits for them, and re-layouts, on_device(): everything[row_tree_nodes]  13.1 us
    dot_general x1, matrix products, on_device(): jnp.dot(gathered_features[node_to_row], projection, preferred_element_typ...  12.6 us
    slice x1, local copies, waits for them, and re-layouts, on_device(): key_value_cache[1]  11.6 us
  transfers between devices with their start and end apart: 11, of which 6 were waited for; matrix products, arithmetic and copies ran while one was open for 16% of the time, Pallas kernels for 0%

profile of v1, /device:TPU:0, one launch (start us, length us, event | category | flops | bytes accessed | tf_op | source)
XLA Modules:
  0.0 347.4 jit_solution(270313036380042734)
XLA Ops:
  7.2 0.8 convert_element_type.39
  8.1 2.8 fusion
  10.9 4.9 %fusion.2 = bf16[256,7168]{1,0:T(8,128)(2,1)} fusion(bf16[256,7168]{1,0:T(8,128)(2,1)} %param.11, f32[7168]{0:T(1024)S(1)} %convert_element_type.39, f32[256]{0:T(256)S(1)} %add_rsqrt_fusion), kind=kLoop, calls=%fused_computation.9 | loop fusion | flops 7340032 | bytes 7369728 | tf_op jit(solution)/shard_map/convert_element_type | solution.py:60
  15.8 1.8 constant_dynamic-slice_fusion.1
  17.7 3.4 fusion.32
  21.1 4.8 %collective-permute-done = bf16[256,8]{0,1:T(8,128)(2,1)S(1)} collective-permute-done((bf16[256,8]{0,1:T(8,128)(2,1)S(1)}, bf16[256,8]{0,1:T(8,128)(2,1)S(1)}, u32[]{:S(2)}, u32[]{:S(2)}) %collective-permute-start) | collective-permute-done | bytes 4128 | tf_op jit(solution)/shard_map/ppermute | solution.py:43
  26.0 3.0 collective-permute-start.4
  28.9 1.3 collective-permute-done.1
  30.2 5.0 %sort.17 = (s32[2048]{0:T(1024)}, s32[2048]{0:T(1024)S(1)}) sort(s32[2048]{0:T(1024)S(1)} %copy-done.3, s32[2048]{0:T(1024)S(1)} %iota.34), dimensions={0}, to_apply=%region_1.2 | sort | flops 22528 | bytes 32768 | tf_op jit(solution)/shard_map/jit(argsort)/sort | solution.py:78
  35.3 3.0 collective-permute-start.5
  38.3 4.5 %copy.22 = bf16[448,3,896]{0,2,1:T(8,128)(2,1)} copy(bf16[448,3,896]{2,0,1:T(8,128)(2,1)} %param.14) | data formatting | bytes 4816896 | tf_op args[3]
  42.8 2.9 collective-permute-start.6
  45.7 1.3 collective-permute-done.6
  47.4 6.2 %gather_fusion.1 = bf16[2048,8]{1,0:T(8,128)(2,1)S(1)} fusion(bf16[2048,8]{1,0:T(8,128)(2,1)S(1)} %copy.23, s32[2048]{0:T(1024)S(1)} %fusion.23), kind=kCustom, calls=%fused_computation.1 | custom fusion | bytes 73728 | tf_op jit(solution)/shard_map/gather | solution.py:84
  53.6 11.1 %gather_fusion = bf16[2048,448]{1,0:T(8,128)(2,1)} fusion(bf16[2048,448]{1,0:T(8,128)(2,1)} %all-gather.3.cloned.1.call-done, s32[2048]{0:T(1024)S(1)} %fusion.23), kind=kCustom, calls=%fused_computation | custom fusion | bytes 3678208 | tf_op jit(solution)/shard_map/gather | solution.py:80
  64.7 12.6 %fusion.31 = f32[2048,2688]{1,0:T(8,128)} fusion(bf16[2048,448]{1,0:T(8,128)(2,1)} %gather_fusion, bf16[448,2688]{0,1:T(8,128)(2,1)} %bitcast.63), kind=kOutput, calls=%fused_computation.88 | convolution fusion | flops 4932501504 | bytes 26263552 | tf_op jit(solution)/shard_map/dot_general | solution.py:79
  77.3 14.3 %convolution_add_fusion = f32[2048,2688]{1,0:T(8,128)} fusion(f32[2048,2688]{1,0:T(8,128)} %fusion.31, bf16[2048,8]{1,0:T(8,128)(2,1)S(1)} %gather_fusion.1, bf16[8,2688]{1,0:T(8,128)(2,1)S(1)} %bitcast.65), kind=kOutput, calls=%fused_computation.4 | convolution fusion | flops 93585408 | bytes 44115968 | tf_op jit(solution)/shard_map/dot_general | solution.py:84
  93.8 10.9 %fusion.28 = (bf16[1,2,2048,896]{3,2,1,0:T(8,128)(2,1)}, bf16[1,2,2048,896]{3,2,1,0:T(8,128)(2,1)}) fusion(bf16[2,2,2048,896]{3,2,1,0:T(8,128)(2,1)} %param.17), kind=kLoop, calls=%fused_computation.85 | loop fusion | bytes 29360128 | tf_op jit(solution)/shard_map/slice | solution.py:100
  104.7 11.3 %copy.25 = bf16[1,2,2048,896]{2,3,1,0:T(8,128)(2,1)} copy(bf16[1,2,2048,896]{3,2,1,0:T(8,128)(2,1)} %get-tuple-element.4) | data formatting | bytes 14680064 | tf_op jit(solution)/shard_map/slice | solution.py:100
  116.0 11.6 %copy.28 = bf16[1,2,2048,896]{2,3,1,0:T(8,128)(2,1)} copy(bf16[1,2,2048,896]{3,2,1,0:T(8,128)(2,1)} %get-tuple-element.5) | data formatting | bytes 14680064 | tf_op jit(solution)/shard_map/slice | solution.py:101
  127.6 102.5 %reduce-scatter.3.cloned.1.call-done = f32[128,2688]{1,0:T(8,128)} async-done(((f32[2048,2688]{1,0:T(8,128)}), f32[128,2688]{1,0:T(8,128)}) %reduce-scatter.3.cloned.1.call-update) | async-done | bytes 1376272 | tf_op jit(solution)/shard_map/reduce_scatter | solution.py:82
  230.1 1.4 convert_element_type.42
  231.6 0.9 reshape.94
  233.0 4.8 %fusion.3 = (f32[2,4,64]{2,1,0:T(4,128)S(1)}, f32[2,4,64,2048]{3,2,1,0:T(8,128)S(1)}) fusion(pred[2,2048]{1,0:T(4,128)(4,1)S(1)} %iota_compare_fusion.3, bf16[2,2048,4,224]{1,3,2,0:T(8,128)(2,1)} %bitcast.59, bf16[2,64,1,4,224]{4,3,2,1,0:T(4,128)(2,1)S(1)} %get-tuple-element.8), kind=kOutput, calls=%fused_computation.13 | convolution fusion | flops 472907264 | bytes 11769856 | tf_op jit(solution)/shard_map/rnhd,rchd->rhnc/dot_general | solution.py:103
  237.9 1.0 fusion.4
  238.9 2.5 fusion.8
  241.9 0.9 reshape.95
  242.9 49.4 %all-gather.5.cloned.1.call-done = bf16[2048,896]{1,0:T(8,128)(2,1)} async-done(((bf16[128,896]{1,0:T(8,128)(2,1)}), bf16[2048,896]{1,0:T(8,128)(2,1)}) %all-gather.5.cloned.1.call-update) | async-done | bytes 3670032 | tf_op jit(solution)/shard_map/all_gather | solution.py:125
  292.2 13.1 %gather_fusion.2 = bf16[2048,896]{1,0:T(8,128)(2,1)} fusion(bf16[2048,896]{1,0:T(8,128)(2,1)} %all-gather.5.cloned.1.call-done, s32[2048]{0:T(1024)S(1)} %fusion.24), kind=kCustom, calls=%fused_computation.2 | custom fusion | bytes 7348224 | tf_op jit(solution)/shard_map/gather | solution.py:128
  305.3 4.3 %convolution_convert_fusion = bf16[2048,224]{0,1:T(8,128)(2,1)} fusion(bf16[2048,896]{1,0:T(8,128)(2,1)} %gather_fusion.2, bf16[896,224]{0,1:T(8,128)(2,1)S(1)} %copy-done.7), kind=kOutput, calls=%fused_computation.15 | convolution fusion | flops 822542336 | bytes 4988928 | tf_op jit(solution)/shard_map/dot_general | solution.py:127
  310.0 0.7 gather_fusion.3
  311.4 29.4 %reduce-scatter.5.cloned.1.call-done = bf16[256,224]{0,1:T(8,128)(2,1)} async-done(((bf16[2048,224]{0,1:T(8,128)(2,1)}), bf16[256,224]{0,1:T(8,128)(2,1)}) %reduce-scatter.5.cloned.1.call-update) | async-done | bytes 114704 | tf_op jit(solution)/shard_map/reduce_scatter | solution.py:126
  (85 shorter events, 5.0 us)
Async XLA Ops:
  7.2 10.5 %copy-start = (bf16[7168,128]{1,0:T(8,128)(2,1)S(1)}, bf16[7168,128]{1,0:T(8,128)(2,1)}, u32[]{:S(2)}) copy-start(bf16[7168,128]{1,0:T(8,128)(2,1)} %param.15) | copy-start | bytes 5505028
  7.2 46.4 %all-gather.3.cloned.1.call-start = ((), (), s32[]{:S(2)}) async-start(), calls=%async_computation.2 | async-start | bytes 2359296 | tf_op jit(solution)/shard_map/all_gather | solution.py:73
  15.8 14.4 %copy-start.3 = (s32[2048]{0:T(1024)S(1)}, s32[2048]{0:T(1024)}, u32[]{:S(2)}) copy-start(s32[2048]{0:T(1024)} %param.12) | copy-start | bytes 24580
  17.6 212.5 %reduce-scatter.3.cloned.1.call-start = ((), (), s32[]{:S(2)}) async-start(), calls=%async_computation.3 | async-start | bytes 23396352 | tf_op jit(solution)/shard_map/reduce_scatter | solution.py:82
  21.1 4.9 %collective-permute-start = (bf16[256,8]{0,1:T(8,128)(2,1)S(1)}, bf16[256,8]{0,1:T(8,128)(2,1)S(1)}, u32[]{:S(2)}, u32[]{:S(2)}) collective-permute-start(bf16[256,8]{0,1:T(8,128)(2,1)S(1)} %dynamic-slice_convert_fusion), channel_id=1, source_target_pairs={{0,16},{16,32},{32,48},{48,64},{64,80},{80,96},{96,112},{112,0},{1... | collective-permute-start | bytes 12296 | tf_op jit(solution)/shard_map/ppermute | solution.py:43
  26.0 4.2 %collective-permute-start.1 = (bf16[256,8]{0,1:T(8,128)(2,1)S(1)}, bf16[256,8]{0,1:T(8,128)(2,1)S(1)}, u32[]{:S(2)}, u32[]{:S(2)}) collective-permute-start(bf16[256,8]{0,1:T(8,128)(2,1)S(1)} %collective-permute-done), channel_id=1, source_target_pairs={{0,16},{16,32},{32,48},{48,64},{64,80},{80,96},{96,112},{112,0},{1... | collective-permute-start | bytes 12296 | tf_op jit(solution)/shard_map/ppermute | solution.py:43
  26.0 9.3 %collective-permute-start.4 = (bf16[256,8]{0,1:T(8,128)(2,1)S(1)}, bf16[256,8]{0,1:T(8,128)(2,1)S(1)}, u32[]{:S(2)}, u32[]{:S(2)}) collective-permute-start(bf16[256,8]{0,1:T(8,128)(2,1)S(1)} %dynamic-slice_convert_fusion), channel_id=1, source_target_pairs={{0,112},{16,0},{32,16},{48,32},{64,48},{80,64},{96,80},{112,96},{1... | collective-permute-start | bytes 12296 | tf_op jit(solution)/shard_map/ppermute | solution.py:45
  30.2 8.0 %collective-permute-start.2 = (bf16[256,8]{0,1:T(8,128)(2,1)S(1)}, bf16[256,8]{0,1:T(8,128)(2,1)S(1)}, u32[]{:S(2)}, u32[]{:S(2)}) collective-permute-start(bf16[256,8]{0,1:T(8,128)(2,1)S(1)} %collective-permute-done.1), channel_id=1, source_target_pairs={{0,16},{16,32},{32,48},{48,64},{64,80},{80,96},{96,112},{112,0},{1... | collective-permute-start | bytes 12296 | tf_op jit(solution)/shard_map/ppermute | solution.py:43
  35.3 7.5 %collective-permute-start.5 = (bf16[256,8]{0,1:T(8,128)(2,1)S(1)}, bf16[256,8]{0,1:T(8,128)(2,1)S(1)}, u32[]{:S(2)}, u32[]{:S(2)}) collective-permute-start(bf16[256,8]{0,1:T(8,128)(2,1)S(1)} %collective-permute-done.4), channel_id=1, source_target_pairs={{0,112},{16,0},{32,16},{48,32},{64,48},{80,64},{96,80},{112,96},{1... | collective-permute-start | bytes 12296 | tf_op jit(solution)/shard_map/ppermute | solution.py:45
  38.2 7.5 %collective-permute-start.3 = (bf16[256,8]{0,1:T(8,128)(2,1)S(1)}, bf16[256,8]{0,1:T(8,128)(2,1)S(1)}, u32[]{:S(2)}, u32[]{:S(2)}) collective-permute-start(bf16[256,8]{0,1:T(8,128)(2,1)S(1)} %collective-permute-done.2), channel_id=1, source_target_pairs={{0,16},{16,32},{32,48},{48,64},{64,80},{80,96},{96,112},{112,0},{1... | collective-permute-start | bytes 12296 | tf_op jit(solution)/shard_map/ppermute | solution.py:43
  42.8 4.2 %collective-permute-start.6 = (bf16[256,8]{0,1:T(8,128)(2,1)S(1)}, bf16[256,8]{0,1:T(8,128)(2,1)S(1)}, u32[]{:S(2)}, u32[]{:S(2)}) collective-permute-start(bf16[256,8]{0,1:T(8,128)(2,1)S(1)} %collective-permute-done.5), channel_id=1, source_target_pairs={{0,112},{16,0},{32,16},{48,32},{64,48},{80,64},{96,80},{112,96},{1... | collective-permute-start | bytes 12296 | tf_op jit(solution)/shard_map/ppermute | solution.py:45
  64.7 12.6 %copy-start.2 = (bf16[8,3,896]{2,0,1:T(8,128)(2,1)S(1)}, bf16[8,3,896]{2,0,1:T(8,128)(2,1)}, u32[]{:S(2)}) copy-start(bf16[8,3,896]{2,0,1:T(8,128)(2,1)} %param.16) | copy-start | bytes 129028
  91.5 0.7 copy-start.4
  91.6 200.7 %all-gather.5.cloned.1.call-start = ((), (), s32[]{:S(2)}) async-start(), calls=%async_computation.4 | async-start | bytes 3899392 | tf_op jit(solution)/shard_map/all_gather | solution.py:125
  116.0 11.6 %copy-start.6 = (s32[2]{0:T(128)S(1)}, s32[2]{0:T(128)}, u32[]{:S(2)}) copy-start(s32[2]{0:T(128)} %param.18) | copy-start | bytes 28
  233.0 6.0 %slice-start = ((s8[7340032]{0:T(1024)(128)(4,1)}), s8[4194304]{0:T(1024)(128)(4,1)S(1)}, s32[]{:S(2)}) async-start(s8[7340032]{0:T(1024)(128)(4,1)} %bitcast.60), calls=%async_computation.6 | async-start | bytes 8388608
  233.0 5.9 %slice-start.1 = ((s8[7340032]{0:T(1024)(128)(4,1)}), s8[3145728]{0:T(1024)(128)(4,1)S(1)}, s32[]{:S(2)}) async-start(s8[7340032]{0:T(1024)(128)(4,1)} %bitcast.60), calls=%async_computation.7 | async-start | bytes 6291456
  242.8 98.1 %reduce-scatter.5.cloned.1.call-start = ((), (), s32[]{:S(2)}) async-start(), calls=%async_computation.5 | async-start | bytes 1032192 | tf_op jit(solution)/shard_map/reduce_scatter | solution.py:126
  242.9 62.5 %copy-start.7 = (bf16[896,224]{0,1:T(8,128)(2,1)S(1)}, bf16[896,224]{0,1:T(8,128)(2,1)}, u32[]{:S(2)}) copy-start(bf16[896,224]{0,1:T(8,128)(2,1)} %param.21) | copy-start | bytes 1204228
  292.2 48.6 %copy-start.1 = (bf16[7168,128]{1,0:T(8,128)(2,1)S(1)}, bf16[7168,128]{1,0:T(8,128)(2,1)}, u32[]{:S(2)}) copy-start(bf16[7168,128]{1,0:T(8,128)(2,1)} %param.15) | copy-start | bytes 5505028
  305.3 4.4 %copy-start.5 = (s32[2,8]{1,0:T(2,128)S(1)}, s32[2,8]{1,0:T(2,128)}, u32[]{:S(2)}) copy-start(s32[2,8]{1,0:T(2,128)} %param.20) | copy-start | bytes 196
Sparse Core Ops, SparseCore 0:
  17.8 28.3 all-gather.2
  91.7 138.4 reduce-scatter.2
  242.9 49.2 all-gather.4
  309.8 31.0 reduce-scatter.4
